TPU v7x, 32 devices: a whole 2x2x4 slice. The times are simulated.
32 devices in a mesh: pa: 8 (over y, x, core), pb: 4 (over z).
Axes of the slice: x: 2, y: 2, z: 4, core: 2. Of those that a mesh axis runs over, the one named last changes fastest.
Arguments:
- queries: bfloat16 [4096, 1024], P(('pa', 'pb')), may hold values from -900 to 900
- batch_hidden: bfloat16 [512, 1024], P(('pa', 'pb')), may hold values from -6 to 6
- pool_hidden: bfloat16 [16384, 1024], P(('pa', 'pb')), may hold values from -6 to 6
- projection: bfloat16 [1024, 1024], replicated, may hold values from -0.1875 to 0.1875
- hard_ids: int32 [4096, 16], P(('pa', 'pb')), may hold values from 0 to 2047, as said below
- query_group: int32 [4096], P(('pa', 'pb')), may hold values from 0 to 63
- labels: int32 [4096], P(('pa', 'pb')), may hold values from 0 to 63
- group_lists: int32 [64, 64], replicated, may hold values from 0 to 127, as said below
Outputs:
- query_grad: bfloat16 [4096, 1024], P(('pa', 'pb'))
- batch_hidden_grad: bfloat16 [512, 1024], P(('pa', 'pb'))
- pool_hidden_grad: bfloat16 [16384, 1024], P(('pa', 'pb'))
Inputs may be any that keep to these rules, and one draw needn't show every extreme that they name: `hard_ids`: entry k of a query's list lies in [(k % 4) * 512, (k % 4 + 1) * 512); entries may repeat. `group_lists`: each row holds 64 different values.
All inputs are finite; a program needn't handle non-finite values.
Results may differ from a plain program's by a relative error of at most 0.017.
The roundings to bfloat16 on the way count: a program that leaves them out, or rounds other values in their place, can miss the bound.
Values may be sent and summed in bfloat16 or wider, within the bound.
No kernel may reach another device: no remote copies, remote signals or barrier semaphores. Data moves between devices by JAX's collectives and lax.ppermute only.
A program may use at most 128 MiB of HBM per device.

v0:
```python
import math
import jax
import jax.numpy as jnp
from jax import lax
from jax.sharding import PartitionSpec as P

D = 1024


def pick_rows(table, wanted):
    flat = wanted.reshape(-1)
    table_iota = lax.broadcasted_iota(jnp.int32, (flat.shape[0], table.shape[0]), 1)
    selector = (flat[:, None] == table_iota).astype(jnp.bfloat16)
    found = jnp.dot(selector, table, preferred_element_type=jnp.float32).astype(table.dtype)
    return found.reshape(wanted.shape + (table.shape[1],))


def add_rows(wanted, values, count):
    flat = wanted.reshape(-1)
    row_iota = lax.broadcasted_iota(jnp.int32, (count, flat.shape[0]), 0)
    selector = (row_iota == flat[None, :]).astype(jnp.bfloat16)
    return jnp.dot(selector, values.reshape(flat.shape[0], -1), preferred_element_type=jnp.float32)


def shards(
    queries, batch_hidden, pool_hidden, projection, hard_ids, query_group, labels, group_lists
):
    score_scale = 1.0 / math.sqrt(D)
    owners = lax.axis_size("pb")
    query_rows = queries.shape[0]
    pool_count = pool_hidden.shape[0]
    hard_count = hard_ids.shape[1]
    per_owner = hard_count // owners
    group_size = group_lists.shape[1]
    group_total = group_lists.shape[0]
    dims = (((1,), (1,)), ((), ()))
    batch_proj = jnp.dot(batch_hidden, projection, preferred_element_type=jnp.float32).astype(
        jnp.bfloat16
    )
    pool_proj = jnp.dot(pool_hidden, projection, preferred_element_type=jnp.float32).astype(
        jnp.bfloat16
    )
    column = lax.all_gather(batch_proj, "pa", axis=0, tiled=True)
    column_count = column.shape[0]
    dense = lax.dot_general(queries, column, dims, preferred_element_type=jnp.float32) * score_scale
    group_iota = lax.broadcasted_iota(jnp.int32, (query_rows, group_total, group_size), 1)
    chosen = jnp.sum(
        jnp.where(query_group[:, None, None] == group_iota, group_lists[None, :, :], 0), axis=1
    )
    column_iota = lax.broadcasted_iota(jnp.int32, (query_rows, group_size, column_count), 2)
    member = chosen[:, :, None] == column_iota
    group_scores = jnp.sum(jnp.where(member, dense[:, None, :], 0.0), axis=2)
    owner_of = lax.broadcasted_iota(jnp.int32, hard_ids.shape, 1) % owners
    local_rows = hard_ids - owner_of * pool_count
    requests = (
        local_rows.reshape(query_rows, per_owner, owners)
        .transpose(2, 0, 1)
        .reshape(owners, query_rows * per_owner)
    )
    received = lax.all_to_all(requests, "pb", split_axis=0, concat_axis=0, tiled=True)
    copies = lax.all_gather(queries, "pb", axis=0, tiled=True).reshape(owners, query_rows, D)
    picked = pick_rows(pool_proj, received).reshape(owners, query_rows, per_owner, D)
    owner_scores = (
        jnp.einsum("sid,sijd->sij", copies, picked, preferred_element_type=jnp.float32)
        * score_scale
    )
    returned = lax.all_to_all(owner_scores, "pb", split_axis=0, concat_axis=0, tiled=True)
    hard_scores = returned.transpose(1, 2, 0).reshape(query_rows, hard_count)
    scores = jnp.concatenate([group_scores, hard_scores], axis=1)
    likely = jax.nn.softmax(scores, axis=1)
    positions = lax.broadcasted_iota(jnp.int32, scores.shape, 1)
    target = (positions == labels[:, None]).astype(jnp.float32)
    dscore = (likely - target).astype(jnp.bfloat16)
    grad_group = dscore[:, :group_size]
    grad_hard = dscore[:, group_size:].reshape(query_rows, per_owner, owners).transpose(2, 0, 1)
    dense_grad = jnp.einsum(
        "ic,icr->ir", grad_group, member.astype(jnp.bfloat16), preferred_element_type=jnp.float32
    ).astype(jnp.bfloat16)
    group_term = jnp.dot(dense_grad, column, preferred_element_type=jnp.float32)
    batch_part = (
        lax.dot_general(
            dense_grad, queries, (((0,), (0,)), ((), ())), preferred_element_type=jnp.float32
        )
        * score_scale
    )
    batch_grad = lax.psum_scatter(batch_part, "pa", scatter_dimension=0, tiled=True)
    sent_back = lax.all_to_all(grad_hard, "pb", split_axis=0, concat_axis=0, tiled=True)
    contrib = (
        score_scale
        * sent_back.astype(jnp.float32)[..., None]
        * copies.astype(jnp.float32)[:, :, None, :]
    )
    contrib = contrib.astype(jnp.bfloat16)
    pool_grad = add_rows(received, contrib, pool_count)
    owner_term = jnp.einsum("sij,sijd->sid", sent_back, picked, preferred_element_type=jnp.float32)
    gathered_terms = lax.all_to_all(owner_term, "pb", split_axis=0, concat_axis=0, tiled=True)
    hard_term = jnp.sum(gathered_terms, axis=0)
    query_grad = (score_scale * (group_term + hard_term)).astype(jnp.bfloat16)
    batch_hidden_grad = lax.dot_general(
        batch_grad.astype(jnp.bfloat16), projection, dims, preferred_element_type=jnp.float32
    ).astype(jnp.bfloat16)
    pool_hidden_grad = lax.dot_general(
        pool_grad.astype(jnp.bfloat16), projection, dims, preferred_element_type=jnp.float32
    ).astype(jnp.bfloat16)
    return (query_grad, batch_hidden_grad, pool_hidden_grad)


def solution(mesh):
    return jax.shard_map(
        shards,
        mesh=mesh,
        in_specs=(
            P(("pa", "pb"), None),
            P(("pa", "pb"), None),
            P(("pa", "pb"), None),
            P(),
            P(("pa", "pb"), None),
            P(("pa", "pb")),
            P(("pa", "pb")),
            P(),
        ),
        out_specs=(P(("pa", "pb"), None), P(("pa", "pb"), None), P(("pa", "pb"), None)),
        check_vma=False,
    )
```

profile of v0, /device:TPU:0, one launch (start us, length us, event | category | flops | bytes accessed | tf_op | source)
XLA Modules:
  0.0 145.6 jit_solution(15382826161694779296)
XLA Ops:
  7.2 0.7 all-gather.2.cloned.1.call-update
  7.9 0.8 multiply_subtract_fusion
  8.7 0.2 copy.23
  8.9 0.8 all_to_all.20
  9.7 6.3 %all-to-all-start = ((s32[4,1,512]{2,1,0:T(1,128)}), s32[4,1,512]{2,1,0:T(1,128)S(1)}, u32[]{:S(2)}, u32[]{:S(2)}) async-start(s32[4,1,512]{2,1,0:T(1,128)} %all_to_all.20), calls=%async_computation | async-start | bytes 16384 | tf_op jit(solution)/shard_map/all_to_all | solution.py:60
  16.0 1.1 convolution_convert_fusion.3
  17.1 9.3 %all_gather.6 = bf16[128,1024]{1,0:T(8,128)(2,1)S(1)} all-gather(bf16[16,1024]{1,0:T(8,128)(2,1)S(1)} %convolution_convert_fusion.3), channel_id=1, replica_groups=mesh['pa'=8,'pb'=4] {'pa'}, dimensions={0}, use_global_device_ids=true | all-gather | bytes 294912 | tf_op jit(solution)/shard_map/all_gather | solution.py:43
  26.4 1.2 fusion.13
  27.6 1.4 select_reduce_fusion.1
  29.3 6.6 %fusion.4 = bf16[2048,1024]{1,0:T(8,128)(2,1)} fusion(s32[2048]{0:T(1024)S(1)} %bitcast.47, bf16[512,1024]{1,0:T(8,128)(2,1)} %param.10, bf16[1024,1024]{1,0:T(8,128)(2,1)S(1)} %copy-done), kind=kOutput, calls=%fused_computation.9 | convolution fusion | flops 3224895488 | bytes 7348224 | tf_op jit(solution)/shard_map/dot_general | solution.py:14
  35.8 7.2 %reshape_reshape.3 = bf16[4,128,4,1024]{3,2,1,0:T(4,128)(2,1)} reshape(bf16[2048,1024]{1,0:T(8,128)(2,1)} %fusion.4) | data formatting | bytes 8388608 | tf_op jit(solution)/shard_map/reshape;reshape | solution.py:62
  43.0 6.8 %fusion.8 = f32[4,128,1,4]{3,2,1,0:T(1,128)S(1)} fusion(bf16[4,128,4,1024]{3,2,1,0:T(4,128)(2,1)} %reshape_reshape.3, bf16[4,128,1024,1]{2,1,0,3:T(8,128)(2,1)} %bitcast.37), kind=kOutput, calls=%fused_computation.16 | convolution fusion | flops 4194304 | bytes 5251072 | tf_op jit(solution)/shard_map/sid,sijd->sij/dot_general | solution.py:64
  49.9 0.6 bitcast_multiply_fusion
  50.6 5.1 %all-to-all-start.1 = ((f32[4,128,4]{1,2,0:T(4,128)}), f32[4,128,4]{1,2,0:T(4,128)S(1)}, u32[]{:S(2)}, u32[]{:S(2)}) async-start(f32[4,128,4]{1,2,0:T(4,128)} %bitcast_multiply_fusion), calls=%async_computation.1 | async-start | bytes 16384 | tf_op jit(solution)/shard_map/all_to_all | solution.py:67
  55.6 2.6 %select_reduce_fusion = f32[128,64]{1,0:T(8,128)S(1)} fusion(f32[128,128]{1,0:T(8,128)S(1)} %copy.22, s32[128,64]{1,0:T(8,128)S(1)} %copy.21), kind=kLoop, calls=%fused_computation.5 | loop fusion | flops 3137536 | bytes 131072 | tf_op jit(solution)/shard_map/reduce_sum | solution.py:52
  58.3 2.9 %all-to-all-done.1 = f32[4,128,4]{1,2,0:T(4,128)S(1)} async-done(((f32[4,128,4]{1,2,0:T(4,128)}), f32[4,128,4]{1,2,0:T(4,128)S(1)}, u32[]{:S(2)}, u32[]{:S(2)}) %all-to-all-start.1) | async-done | bytes 8224 | tf_op jit(solution)/shard_map/all_to_all | solution.py:67
  61.4 0.2 fusion.19
  61.9 7.9 %all_to_all.25 = bf16[4,128,4]{1,2,0:T(4,128)(2,1)S(1)} all-to-all(bf16[4,128,4]{1,2,0:T(4,128)(2,1)S(1)} %copy.28), channel_id=1, replica_groups=mesh['pa'=8,'pb'=4] {'pb'}, dimensions={0} | all-to-all | bytes 8192 | tf_op jit(solution)/shard_map/all_to_all | solution.py:87
  69.8 0.2 copy.34
  70.0 4.5 %fusion.20 = f32[4,128,1,1024]{3,2,1,0:T(1,128)S(1)} fusion(bf16[4,128,4,1]{2,3,1,0:T(2,128)(2,1)S(1)} %copy.34, bf16[4,128,4,1024]{3,2,1,0:T(4,128)(2,1)} %reshape_reshape.3), kind=kOutput, calls=%fused_computation.45 | convolution fusion | flops 4194304 | bytes 6295552 | tf_op jit(solution)/shard_map/sij,sijd->sid/dot_general | solution.py:95
  74.5 1.8 %copy.41 = f32[4,128,1,1024]{3,1,0,2:T(8,128)} copy(f32[4,128,1,1024]{3,2,1,0:T(1,128)S(1)} %fusion.20) | data formatting | bytes 4194304 | tf_op jit(solution)/shard_map/sij,sijd->sid/dot_general | solution.py:95
  76.3 4.4 %all-to-all-start.3 = ((f32[4,128,1024]{2,1,0:T(8,128)}), f32[4,128,1024]{2,1,0:T(8,128)}, u32[]{:S(2)}, u32[]{:S(2)}) async-start(f32[4,128,1024]{2,1,0:T(8,128)} %bitcast.36), calls=%async_computation.3 | async-start | bytes 4194304 | tf_op jit(solution)/shard_map/all_to_all | solution.py:96
  80.8 5.5 %mul.62 = f32[4,128,4,1024]{3,2,1,0:T(4,128)} broadcast(bf16[4,128,1024]{2,1,0:T(8,128)(2,1)S(1)} %bitcast.38), dimensions={0,1,3} | broadcast | bytes 9437184 | tf_op jit(solution)/shard_map/mul | solution.py:89
  86.3 10.0 %mul.63 = f32[2048,1024]{1,0:T(8,128)} reshape(f32[4,128,4,1024]{3,2,1,0:T(4,128)} %mul.62) | data formatting | bytes 16777216 | tf_op jit(solution)/shard_map/mul | solution.py:89
  96.3 1.8 %fusion.2 = f32[128,1,128]{2,1,0:T(1,128)S(1)} fusion(s32[128,64]{1,0:T(8,128)S(1)} %copy.21, bf16[128,64,1]{1,0,2:T(8,128)(2,1)S(1)} %slice_bitcast_fusion), kind=kOutput, calls=%fused_computation.7 | convolution fusion | flops 3145728 | bytes 114688 | tf_op jit(solution)/shard_map/ic,icr->ir/dot_general | solution.py:76
  98.1 1.1 convolution_multiply_fusion
  99.4 0.2 mul.60
  99.6 7.9 %convolution_convert_fusion = bf16[512,1024]{1,0:T(8,128)(2,1)} fusion(bf16[1024,1024]{1,0:T(8,128)(2,1)S(1)} %copy-done, f32[2048,1024]{1,0:T(8,128)} %mul.63, f32[2048]{0:T(1024)S(1)} %mul.60, s32[2048]{0:T(1024)S(1)} %bitcast.48), kind=kOutput, calls=%fused_computation.19 | convolution fusion | flops 3227516928 | bytes 11550720 | tf_op jit(solution)/shard_map/dot_general | solution.py:102
  107.5 26.5 %reduce-scatter.2.cloned.1.call-done = f32[16,1024]{1,0:T(8,128)} async-done(((f32[128,1024]{1,0:T(8,128)}), f32[16,1024]{1,0:T(8,128)}) %reduce-scatter.2.cloned.1.call-update) | async-done | bytes 65552 | tf_op jit(solution)/shard_map/reduce_scatter | solution.py:86
  133.9 2.1 %convolution_convert_fusion.2 = bf16[16,1024]{1,0:T(8,128)(2,1)} fusion(bf16[1024,1024]{1,0:T(8,128)(2,1)S(1)} %copy-done, f32[16,1024]{1,0:T(8,128)} %reduce-scatter.2.cloned.1.call-done), kind=kOutput, calls=%fused_computation.27 | convolution fusion | flops 33587200 | bytes 2195456 | tf_op jit(solution)/shard_map/dot_general | solution.py:99
  136.1 1.8 %reduce_sum.39 = f32[128,1024]{1,0:T(8,128)S(1)} reduce(f32[4,128,1024]{2,1,0:T(8,128)} %all-to-all-done.3, f32[]{:T(128)} %constant.11.clone.1), dimensions={0}, to_apply=%region_5.6 | reduce | flops 393216 | bytes 2621444 | tf_op jit(solution)/shard_map/reduce_sum | solution.py:97
  137.9 0.9 fusion.12
  (31 shorter events, 1.1 us)
Async XLA Ops:
  7.2 8.8 %copy-start = (bf16[1024,1024]{1,0:T(8,128)(2,1)S(1)}, bf16[1024,1024]{1,0:T(8,128)(2,1)}, u32[]{:S(2)}) copy-start(bf16[1024,1024]{1,0:T(8,128)(2,1)} %param.11) | copy-start | bytes 6291460
  7.2 35.9 %all-gather.2.cloned.1.call-start = ((), (), s32[]{:S(2)}) async-start(), calls=%async_computation.5 | async-start | bytes 1310720 | tf_op jit(solution)/shard_map/all_gather | solution.py:61
  9.7 19.6 %all-to-all-start = ((s32[4,1,512]{2,1,0:T(1,128)}), s32[4,1,512]{2,1,0:T(1,128)S(1)}, u32[]{:S(2)}, u32[]{:S(2)}) async-start(s32[4,1,512]{2,1,0:T(1,128)} %all_to_all.20), calls=%async_computation | async-start | bytes 16384 | tf_op jit(solution)/shard_map/all_to_all | solution.py:60
  43.0 18.5 %copy-start.3 = (s32[128]{0:T(128)S(1)}, s32[128]{0:T(128)}, u32[]{:S(2)}) copy-start(s32[128]{0:T(128)} %param.14) | copy-start | bytes 1540
  50.6 10.7 %all-to-all-start.1 = ((f32[4,128,4]{1,2,0:T(4,128)}), f32[4,128,4]{1,2,0:T(4,128)S(1)}, u32[]{:S(2)}, u32[]{:S(2)}) async-start(f32[4,128,4]{1,2,0:T(4,128)} %bitcast_multiply_fusion), calls=%async_computation.1 | async-start | bytes 16384 | tf_op jit(solution)/shard_map/all_to_all | solution.py:67
  74.5 6.3 %copy-start.2 = (bf16[512,1024]{1,0:T(8,128)(2,1)S(1)}, bf16[512,1024]{1,0:T(8,128)(2,1)}, u32[]{:S(2)}) copy-start(bf16[512,1024]{1,0:T(8,128)(2,1)} %all-gather.2.cloned.1.call-done) | copy-start | bytes 3145732
  76.3 59.8 %all-to-all-start.3 = ((f32[4,128,1024]{2,1,0:T(8,128)}), f32[4,128,1024]{2,1,0:T(8,128)}, u32[]{:S(2)}, u32[]{:S(2)}) async-start(f32[4,128,1024]{2,1,0:T(8,128)} %bitcast.36), calls=%async_computation.3 | async-start | bytes 4194304 | tf_op jit(solution)/shard_map/all_to_all | solution.py:96
  80.7 53.2 %reduce-scatter.2.cloned.1.call-start = ((), (), s32[]{:S(2)}) async-start(), calls=%async_computation.6 | async-start | bytes 589824 | tf_op jit(solution)/shard_map/reduce_scatter | solution.py:86
  86.3 11.8 %copy-start.1 = (bf16[128,1024]{1,0:T(8,128)(2,1)S(1)}, bf16[128,1024]{1,0:T(8,128)(2,1)}, u32[]{:S(2)}) copy-start(bf16[128,1024]{1,0:T(8,128)(2,1)} %param.8) | copy-start | bytes 786436
Sparse Core Ops, SparseCore 0:
  9.6 30.6 all-gather.1
  99.4 34.5 reduce-scatter.1
where the time goes:
time: 147 us; the launch traced here: 146 us
  matrix products  34 us (23%)
  waiting for transfers between devices  30.1 us (20%)
  local copies, waits for them, and re-layouts  26.5 us (18%)
  blocking collectives  17.2 us (12%)
  starting transfers between devices  16 us (11%)
  between operations  14.2 us (10%)
  other arithmetic  7.67 us (5%)
    reduce_scatter x1, waiting for transfers between devices, shards(): lax.psum_scatter(batch_part, 'pa', scatter_dimension=0, tiled=True)  26.5 us
    mul x4, local copies, waits for them, and re-layouts, shards(): score_scale * sent_back.astype(jnp.float32)[..., None]  15.8 us
    all_gather x1, blocking collectives, shards(): column = lax.all_gather(batch_proj, 'pa', axis=0, tiled=True)  9.29 us
    all_to_all x1, blocking collectives, shards(): lax.all_to_all(grad_hard, 'pb', split_axis=0, concat_axis=0, tiled=True)  7.94 us
    dot_general x1, matrix products, shards(): lax.dot_general(pool_grad.astype(jnp.bfloat16), projection, dims, preferr...  7.86 us
    another operation x1, local copies, waits for them, and re-layouts, shards(): pick_rows(pool_proj, received).reshape(owners, query_rows, per_owner, D)  7.2 us
    dot_general x1, matrix products, shards(): jnp.einsum('sid,sijd->sij', copies, picked, preferred_element_type=jnp.fl...  6.77 us
    dot_general x1, matrix products, pick_rows(): jnp.dot(selector, table, preferred_element_type=jnp.float32)  6.57 us
  transfers between devices with their start and end apart: 5, of which 2 were waited for; matrix products, arithmetic and copies ran while one was open for 34% of the time, Pallas kernels for 0%

commit v1 on v0

--- a/solution.py
+++ b/solution.py
@@ -5,6 +5,27 @@
 from jax.sharding import PartitionSpec as P
 
 D = 1024
+
+
+def gather_around(array, axis, dim):
+    length, index, width = (lax.axis_size(axis), lax.axis_index(axis), array.shape[dim])
+    right = [(i, (i + 1) % length) for i in range(length)]
+    behind = [(i, (i - 1) % length) for i in range(length)]
+    whole = jnp.zeros((*array.shape[:dim], length * width, *array.shape[dim + 1 :]), array.dtype)
+    whole = lax.dynamic_update_slice_in_dim(whole, array, index * width, axis=dim)
+    from_left = from_right = array
+    half = length // 2
+    for step in range(1, half + 1):
+        from_left = lax.ppermute(from_left, axis, right)
+        whole = lax.dynamic_update_slice_in_dim(
+            whole, from_left, (index - step) % length * width, axis=dim
+        )
+        if step < length - half:
+            from_right = lax.ppermute(from_right, axis, behind)
+            whole = lax.dynamic_update_slice_in_dim(
+                whole, from_right, (index + step) % length * width, axis=dim
+            )
+    return whole
 
 
 def pick_rows(table, wanted):
@@ -40,7 +61,7 @@
     pool_proj = jnp.dot(pool_hidden, projection, preferred_element_type=jnp.float32).astype(
         jnp.bfloat16
     )
-    column = lax.all_gather(batch_proj, "pa", axis=0, tiled=True)
+    column = gather_around(batch_proj, "pa", 0)
     column_count = column.shape[0]
     dense = lax.dot_general(queries, column, dims, preferred_element_type=jnp.float32) * score_scale
     group_iota = lax.broadcasted_iota(jnp.int32, (query_rows, group_total, group_size), 1)

time: 147 us -> 157 us (1.068)
  waiting for transfers between devices: 30.1 us -> 40.6 us
  blocking collectives: 17.2 us -> 7.94 us
  starting transfers between devices: 16 us -> 22.4 us
  local copies, waits for them, and re-layouts: 26.5 us -> 29.4 us
    all_gather x1 -> x0, blocking collectives: 9.29 us -> none  [shards(): column = lax.all_gather(batch_proj, 'pa', axis=0, tiled=True)]
    ppermute x0 -> x7, starting transfers between devices: none -> 9.07 us  [the longest x3 8.57 us: gather_around(): from_right = lax.ppermute(from_right, axis, behind)]
    ppermute x0 -> x7, waiting for transfers between devices: none -> 6.99 us  [the longest x4 6.58 us: gather_around(): from_left = lax.ppermute(from_left, axis, right)]
    all_to_all x1, waiting for transfers between devices: 0.01 us -> 3.19 us  [shards(): lax.all_to_all(requests, 'pb', split_axis=0, concat_axis=0, tiled=True)]
    all_to_all x1, starting transfers between devices: 5.09 us -> 3.25 us  [shards(): lax.all_to_all(owner_scores, 'pb', split_axis=0, concat_axis=0, tiled=True)]
  transfers between devices with their start and end apart: 5 -> 12, of which waited for: 2 -> 7; matrix products, arithmetic and copies ran while one was open for 34% -> 32% of each run, Pallas kernels for 0% -> 0%
where the time goes in v1:
time: 157 us; the launch traced here: 155 us
  waiting for transfers between devices  40.6 us (26%)
  matrix products  33 us (21%)
  local copies, waits for them, and re-layouts  29.4 us (19%)
  starting transfers between devices  22.4 us (14%)
  between operations  14.4 us (9%)
  blocking collectives  7.94 us (5%)
  other arithmetic  7.68 us (5%)
    reduce_scatter x1, waiting for transfers between devices, shards(): lax.psum_scatter(batch_part, 'pa', scatter_dimension=0, tiled=True)  26.8 us
    mul x4, local copies, waits for them, and re-layouts, shards(): score_scale * sent_back.astype(jnp.float32)[..., None]  17 us
    ppermute x3, starting transfers between devices, gather_around(): from_right = lax.ppermute(from_right, axis, behind)  8.57 us
    all_to_all x1, blocking collectives, shards(): lax.all_to_all(grad_hard, 'pb', split_axis=0, concat_axis=0, tiled=True)  7.94 us
    dot_general x1, matrix products, shards(): lax.dot_general(pool_grad.astype(jnp.bfloat16), projection, dims, preferr...  7.86 us
    another operation x1, local copies, waits for them, and re-layouts, shards(): pick_rows(pool_proj, received).reshape(owners, query_rows, per_owner, D)  7.26 us
    dot_general x1, matrix products, shards(): jnp.einsum('sid,sijd->sij', copies, picked, preferred_element_type=jnp.fl...  6.77 us
    dot_general x1, matrix products, pick_rows(): jnp.dot(selector, table, preferred_element_type=jnp.float32)  6.59 us
  transfers between devices with their start and end apart: 12, of which 7 were waited for; matrix products, arithmetic and copies ran while one was open for 32% of the time, Pallas kernels for 0%

profile of v1, /device:TPU:0, one launch (start us, length us, event | category | flops | bytes accessed | tf_op | source)
XLA Modules:
  0.0 155.4 jit_solution(15289292224177315846)
XLA Ops:
  7.2 1.5 copy-done
  8.8 1.1 constant_dynamic-update-slice_fusion.7
  10.4 2.9 %collective-permute-start.1 = (bf16[16,1024]{1,0:T(8,128)(2,1)S(1)}, bf16[16,1024]{1,0:T(8,128)(2,1)S(1)}, u32[]{:S(2)}, u32[]{:S(2)}) collective-permute-start(bf16[16,1024]{1,0:T(8,128)(2,1)S(1)} %get-tuple-element.4), channel_id=1, source_target_pairs={{0,28},{4,0},{8,4},{12,8},{16,12},{20,16},{24,20},{28,24},{1,29},{... | collective-permute-start | bytes 98312 | tf_op jit(solution)/shard_map/ppermute | solution.py:24
  13.3 0.8 multiply_subtract_fusion
  14.2 0.8 all_to_all.20
  15.0 5.6 %all-to-all-start = ((s32[4,1,512]{2,1,0:T(1,128)}), s32[4,1,512]{2,1,0:T(1,128)S(1)}, u32[]{:S(2)}, u32[]{:S(2)}) async-start(s32[4,1,512]{2,1,0:T(1,128)} %all_to_all.20), calls=%async_computation | async-start | bytes 16384 | tf_op jit(solution)/shard_map/all_to_all | solution.py:81
  21.3 1.4 select_reduce_fusion.1
  23.0 3.2 %all-to-all-done = s32[4,1,512]{2,1,0:T(1,128)S(1)} async-done(((s32[4,1,512]{2,1,0:T(1,128)}), s32[4,1,512]{2,1,0:T(1,128)S(1)}, u32[]{:S(2)}, u32[]{:S(2)}) %all-to-all-start) | async-done | bytes 8224 | tf_op jit(solution)/shard_map/all_to_all | solution.py:81
  26.2 6.6 %fusion.4 = bf16[2048,1024]{1,0:T(8,128)(2,1)} fusion(s32[2048]{0:T(1024)S(1)} %bitcast.47, bf16[512,1024]{1,0:T(8,128)(2,1)} %param.10, bf16[1024,1024]{1,0:T(8,128)(2,1)S(1)} %copy-done), kind=kOutput, calls=%fused_computation.9 | convolution fusion | flops 3224895488 | bytes 7348224 | tf_op jit(solution)/shard_map/dot_general | solution.py:35
  32.8 7.3 %reshape_reshape.3 = bf16[4,128,4,1024]{3,2,1,0:T(4,128)(2,1)} reshape(bf16[2048,1024]{1,0:T(8,128)(2,1)} %fusion.4) | data formatting | bytes 8388608 | tf_op jit(solution)/shard_map/reshape;reshape | solution.py:83
  40.1 2.6 %collective-permute-start.3 = (bf16[16,1024]{1,0:T(8,128)(2,1)S(1)}, bf16[16,1024]{1,0:T(8,128)(2,1)S(1)}, u32[]{:S(2)}, u32[]{:S(2)}) collective-permute-start(bf16[16,1024]{1,0:T(8,128)(2,1)S(1)} %collective-permute-done.1), channel_id=1, source_target_pairs={{0,28},{4,0},{8,4},{12,8},{16,12},{20,16},{24,20},{28,24},{1,29},{... | collective-permute-start | bytes 98312 | tf_op jit(solution)/shard_map/ppermute | solution.py:24
  42.7 1.6 %collective-permute-done.2 = bf16[16,1024]{1,0:T(8,128)(2,1)S(1)} collective-permute-done((bf16[16,1024]{1,0:T(8,128)(2,1)S(1)}, bf16[16,1024]{1,0:T(8,128)(2,1)S(1)}, u32[]{:S(2)}, u32[]{:S(2)}) %collective-permute-start.2) | collective-permute-done | bytes 32800 | tf_op jit(solution)/shard_map/ppermute | solution.py:19
  44.3 3.0 %collective-permute-start.5 = (bf16[16,1024]{1,0:T(8,128)(2,1)S(1)}, bf16[16,1024]{1,0:T(8,128)(2,1)S(1)}, u32[]{:S(2)}, u32[]{:S(2)}) collective-permute-start(bf16[16,1024]{1,0:T(8,128)(2,1)S(1)} %collective-permute-done.3), channel_id=1, source_target_pairs={{0,28},{4,0},{8,4},{12,8},{16,12},{20,16},{24,20},{28,24},{1,29},{... | collective-permute-start | bytes 98312 | tf_op jit(solution)/shard_map/ppermute | solution.py:24
  47.4 1.2 collective-permute-done.4
  49.0 3.8 %collective-permute-done.6 = bf16[16,1024]{1,0:T(8,128)(2,1)S(1)} collective-permute-done((bf16[16,1024]{1,0:T(8,128)(2,1)S(1)}, bf16[16,1024]{1,0:T(8,128)(2,1)S(1)}, u32[]{:S(2)}, u32[]{:S(2)}) %collective-permute-start.6) | collective-permute-done | bytes 32800 | tf_op jit(solution)/shard_map/ppermute | solution.py:19
  53.2 6.8 %fusion.8 = f32[4,128,1,4]{3,2,1,0:T(1,128)S(1)} fusion(bf16[4,128,4,1024]{3,2,1,0:T(4,128)(2,1)} %reshape_reshape.3, bf16[4,128,1024,1]{2,1,0,3:T(8,128)(2,1)} %bitcast.37), kind=kOutput, calls=%fused_computation.16 | convolution fusion | flops 4194304 | bytes 5251072 | tf_op jit(solution)/shard_map/sid,sijd->sij/dot_general | solution.py:85
  60.7 3.2 %all-to-all-start.1 = ((f32[4,128,4]{1,2,0:T(4,128)}), f32[4,128,4]{1,2,0:T(4,128)S(1)}, u32[]{:S(2)}, u32[]{:S(2)}) async-start(f32[4,128,4]{1,2,0:T(4,128)} %bitcast_multiply_fusion), calls=%async_computation.1 | async-start | bytes 16384 | tf_op jit(solution)/shard_map/all_to_all | solution.py:88
  63.9 2.6 %select_reduce_fusion = f32[128,64]{1,0:T(8,128)S(1)} fusion(f32[128,128]{1,0:T(8,128)S(1)} %copy.22, s32[128,64]{1,0:T(8,128)S(1)} %copy.21), kind=kLoop, calls=%fused_computation.5 | loop fusion | flops 3137536 | bytes 131072 | tf_op jit(solution)/shard_map/reduce_sum | solution.py:73
  66.6 2.8 %all-to-all-done.1 = f32[4,128,4]{1,2,0:T(4,128)S(1)} async-done(((f32[4,128,4]{1,2,0:T(4,128)}), f32[4,128,4]{1,2,0:T(4,128)S(1)}, u32[]{:S(2)}, u32[]{:S(2)}) %all-to-all-start.1) | async-done | bytes 8224 | tf_op jit(solution)/shard_map/all_to_all | solution.py:88
  70.1 7.9 %all_to_all.25 = bf16[4,128,4]{1,2,0:T(4,128)(2,1)S(1)} all-to-all(bf16[4,128,4]{1,2,0:T(4,128)(2,1)S(1)} %copy.28), channel_id=1, replica_groups=mesh['pa'=8,'pb'=4] {'pb'}, dimensions={0} | all-to-all | bytes 8192 | tf_op jit(solution)/shard_map/all_to_all | solution.py:108
  78.3 4.5 %fusion.20 = f32[4,128,1,1024]{3,2,1,0:T(1,128)S(1)} fusion(bf16[4,128,4,1]{2,3,1,0:T(2,128)(2,1)S(1)} %copy.34, bf16[4,128,4,1024]{3,2,1,0:T(4,128)(2,1)} %reshape_reshape.3), kind=kOutput, calls=%fused_computation.53 | convolution fusion | flops 4194304 | bytes 6295552 | tf_op jit(solution)/shard_map/sij,sijd->sid/dot_general | solution.py:116
  82.8 1.8 %copy.41 = f32[4,128,1,1024]{3,1,0,2:T(8,128)} copy(f32[4,128,1,1024]{3,2,1,0:T(1,128)S(1)} %fusion.20) | data formatting | bytes 4194304 | tf_op jit(solution)/shard_map/sij,sijd->sid/dot_general | solution.py:116
  84.5 4.4 %all-to-all-start.3 = ((f32[4,128,1024]{2,1,0:T(8,128)}), f32[4,128,1024]{2,1,0:T(8,128)}, u32[]{:S(2)}, u32[]{:S(2)}) async-start(f32[4,128,1024]{2,1,0:T(8,128)} %bitcast.36), calls=%async_computation.3 | async-start | bytes 4194304 | tf_op jit(solution)/shard_map/all_to_all | solution.py:117
  89.0 6.7 %mul.94 = f32[4,128,4,1024]{3,2,1,0:T(4,128)} broadcast(bf16[4,128,1024]{2,1,0:T(8,128)(2,1)} %bitcast.38), dimensions={0,1,3} | broadcast | bytes 9437184 | tf_op jit(solution)/shard_map/mul | solution.py:110
  95.8 10.0 %mul.95 = f32[2048,1024]{1,0:T(8,128)} reshape(f32[4,128,4,1024]{3,2,1,0:T(4,128)} %mul.94) | data formatting | bytes 16777216 | tf_op jit(solution)/shard_map/mul | solution.py:110
  105.8 1.8 %fusion.2 = f32[128,1,128]{2,1,0:T(1,128)S(1)} fusion(s32[128,64]{1,0:T(8,128)S(1)} %copy.21, bf16[128,64,1]{1,0,2:T(8,128)(2,1)S(1)} %slice_bitcast_fusion), kind=kOutput, calls=%fused_computation.7 | convolution fusion | flops 3145728 | bytes 114688 | tf_op jit(solution)/shard_map/ic,icr->ir/dot_general | solution.py:97
  107.6 1.1 convolution_multiply_fusion
  109.0 7.9 %convolution_convert_fusion = bf16[512,1024]{1,0:T(8,128)(2,1)} fusion(bf16[1024,1024]{1,0:T(8,128)(2,1)S(1)} %copy-done, f32[2048,1024]{1,0:T(8,128)} %mul.95, f32[2048]{0:T(1024)S(1)} %mul.92, s32[2048]{0:T(1024)S(1)} %bitcast.48), kind=kOutput, calls=%fused_computation.19 | convolution fusion | flops 3227516928 | bytes 11550720 | tf_op jit(solution)/shard_map/dot_general | solution.py:123
  116.9 26.8 %reduce-scatter.2.cloned.1.call-done = f32[16,1024]{1,0:T(8,128)} async-done(((f32[128,1024]{1,0:T(8,128)}), f32[16,1024]{1,0:T(8,128)}) %reduce-scatter.2.cloned.1.call-update) | async-done | bytes 65552 | tf_op jit(solution)/shard_map/reduce_scatter | solution.py:107
  143.7 2.1 %convolution_convert_fusion.2 = bf16[16,1024]{1,0:T(8,128)(2,1)} fusion(bf16[1024,1024]{1,0:T(8,128)(2,1)S(1)} %copy-done, f32[16,1024]{1,0:T(8,128)} %reduce-scatter.2.cloned.1.call-done), kind=kOutput, calls=%fused_computation.27 | convolution fusion | flops 33587200 | bytes 2195456 | tf_op jit(solution)/shard_map/dot_general | solution.py:120
  145.8 1.8 %reduce_sum.39 = f32[128,1024]{1,0:T(8,128)S(1)} reduce(f32[4,128,1024]{2,1,0:T(8,128)} %all-to-all-done.3, f32[]{:T(128)} %constant.86.clone.1), dimensions={0}, to_apply=%region_5.6 | reduce | flops 393216 | bytes 2621444 | tf_op jit(solution)/shard_map/reduce_sum | solution.py:118
  147.6 0.9 fusion.12
  (50 shorter events, 4.3 us)
Async XLA Ops:
  7.2 1.6 %copy-start = (bf16[1024,1024]{1,0:T(8,128)(2,1)S(1)}, bf16[1024,1024]{1,0:T(8,128)(2,1)}, u32[]{:S(2)}) copy-start(bf16[1024,1024]{1,0:T(8,128)(2,1)} %param.11) | copy-start | bytes 6291460
  9.9 30.2 %collective-permute-start = (bf16[16,1024]{1,0:T(8,128)(2,1)S(1)}, bf16[16,1024]{1,0:T(8,128)(2,1)S(1)}, u32[]{:S(2)}, u32[]{:S(2)}) collective-permute-start(bf16[16,1024]{1,0:T(8,128)(2,1)S(1)} %get-tuple-element.4), channel_id=1, source_target_pairs={{0,4},{4,8},{8,12},{12,16},{16,20},{20,24},{24,28},{28,0},{1,5},{5... | collective-permute-start | bytes 98312 | tf_op jit(solution)/shard_map/ppermute | solution.py:19
  10.4 29.7 %collective-permute-start.1 = (bf16[16,1024]{1,0:T(8,128)(2,1)S(1)}, bf16[16,1024]{1,0:T(8,128)(2,1)S(1)}, u32[]{:S(2)}, u32[]{:S(2)}) collective-permute-start(bf16[16,1024]{1,0:T(8,128)(2,1)S(1)} %get-tuple-element.4), channel_id=1, source_target_pairs={{0,28},{4,0},{8,4},{12,8},{16,12},{20,16},{24,20},{28,24},{1,29},{... | collective-permute-start | bytes 98312 | tf_op jit(solution)/shard_map/ppermute | solution.py:24
  15.0 11.2 %all-to-all-start = ((s32[4,1,512]{2,1,0:T(1,128)}), s32[4,1,512]{2,1,0:T(1,128)S(1)}, u32[]{:S(2)}, u32[]{:S(2)}) async-start(s32[4,1,512]{2,1,0:T(1,128)} %all_to_all.20), calls=%async_computation | async-start | bytes 16384 | tf_op jit(solution)/shard_map/all_to_all | solution.py:81
  20.6 32.5 %all-gather.2.cloned.1.call-start = ((), (), s32[]{:S(2)}) async-start(), calls=%async_computation.5 | async-start | bytes 1310720 | tf_op jit(solution)/shard_map/all_gather | solution.py:82
  32.8 20.0 %copy-start.1 = (bf16[128,1024]{1,0:T(8,128)(2,1)S(1)}, bf16[128,1024]{1,0:T(8,128)(2,1)}, u32[]{:S(2)}) copy-start(bf16[128,1024]{1,0:T(8,128)(2,1)} %param.8) | copy-start | bytes 786436
  40.1 4.2 %collective-permute-start.2 = (bf16[16,1024]{1,0:T(8,128)(2,1)S(1)}, bf16[16,1024]{1,0:T(8,128)(2,1)S(1)}, u32[]{:S(2)}, u32[]{:S(2)}) collective-permute-start(bf16[16,1024]{1,0:T(8,128)(2,1)S(1)} %collective-permute-done), channel_id=1, source_target_pairs={{0,4},{4,8},{8,12},{12,16},{16,20},{20,24},{24,28},{28,0},{1,5},{5... | collective-permute-start | bytes 98312 | tf_op jit(solution)/shard_map/ppermute | solution.py:19
  40.1 4.2 %collective-permute-start.3 = (bf16[16,1024]{1,0:T(8,128)(2,1)S(1)}, bf16[16,1024]{1,0:T(8,128)(2,1)S(1)}, u32[]{:S(2)}, u32[]{:S(2)}) collective-permute-start(bf16[16,1024]{1,0:T(8,128)(2,1)S(1)} %collective-permute-done.1), channel_id=1, source_target_pairs={{0,28},{4,0},{8,4},{12,8},{16,12},{20,16},{24,20},{28,24},{1,29},{... | collective-permute-start | bytes 98312 | tf_op jit(solution)/shard_map/ppermute | solution.py:24
  44.3 4.2 %collective-permute-start.4 = (bf16[16,1024]{1,0:T(8,128)(2,1)S(1)}, bf16[16,1024]{1,0:T(8,128)(2,1)S(1)}, u32[]{:S(2)}, u32[]{:S(2)}) collective-permute-start(bf16[16,1024]{1,0:T(8,128)(2,1)S(1)} %collective-permute-done.2), channel_id=1, source_target_pairs={{0,4},{4,8},{8,12},{12,16},{16,20},{20,24},{24,28},{28,0},{1,5},{5... | collective-permute-start | bytes 98312 | tf_op jit(solution)/shard_map/ppermute | solution.py:19
  44.3 4.6 %collective-permute-start.5 = (bf16[16,1024]{1,0:T(8,128)(2,1)S(1)}, bf16[16,1024]{1,0:T(8,128)(2,1)S(1)}, u32[]{:S(2)}, u32[]{:S(2)}) collective-permute-start(bf16[16,1024]{1,0:T(8,128)(2,1)S(1)} %collective-permute-done.3), channel_id=1, source_target_pairs={{0,28},{4,0},{8,4},{12,8},{16,12},{20,16},{24,20},{28,24},{1,29},{... | collective-permute-start | bytes 98312 | tf_op jit(solution)/shard_map/ppermute | solution.py:24
  48.5 4.2 %collective-permute-start.6 = (bf16[16,1024]{1,0:T(8,128)(2,1)S(1)}, bf16[16,1024]{1,0:T(8,128)(2,1)S(1)}, u32[]{:S(2)}, u32[]{:S(2)}) collective-permute-start(bf16[16,1024]{1,0:T(8,128)(2,1)S(1)} %collective-permute-done.4), channel_id=1, source_target_pairs={{0,4},{4,8},{8,12},{12,16},{16,20},{20,24},{24,28},{28,0},{1,5},{5... | collective-permute-start | bytes 98312 | tf_op jit(solution)/shard_map/ppermute | solution.py:19
  53.2 16.7 %copy-start.2 = (s32[128]{0:T(128)S(1)}, s32[128]{0:T(128)}, u32[]{:S(2)}) copy-start(s32[128]{0:T(128)} %param.14) | copy-start | bytes 1540
  60.7 8.8 %all-to-all-start.1 = ((f32[4,128,4]{1,2,0:T(4,128)}), f32[4,128,4]{1,2,0:T(4,128)S(1)}, u32[]{:S(2)}, u32[]{:S(2)}) async-start(f32[4,128,4]{1,2,0:T(4,128)} %bitcast_multiply_fusion), calls=%async_computation.1 | async-start | bytes 16384 | tf_op jit(solution)/shard_map/all_to_all | solution.py:88
  84.5 61.3 %all-to-all-start.3 = ((f32[4,128,1024]{2,1,0:T(8,128)}), f32[4,128,1024]{2,1,0:T(8,128)}, u32[]{:S(2)}, u32[]{:S(2)}) async-start(f32[4,128,1024]{2,1,0:T(8,128)} %bitcast.36), calls=%async_computation.3 | async-start | bytes 4194304 | tf_op jit(solution)/shard_map/all_to_all | solution.py:117
  89.0 54.7 %reduce-scatter.2.cloned.1.call-start = ((), (), s32[]{:S(2)}) async-start(), calls=%async_computation.6 | async-start | bytes 589824 | tf_op jit(solution)/shard_map/reduce_scatter | solution.py:107
Sparse Core Ops, SparseCore 0:
  23.0 28.5 all-gather.1
  108.8 34.8 reduce-scatter.1
